TPU v7x, 256 devices: a whole 4x4x8 slice. The times are simulated.
256 devices in a mesh: tm: 16 (over z, core), panel: 16 (over y, x).
Axes of the slice: x: 4, y: 4, z: 8, core: 2. Of those that a mesh axis runs over, the one named last changes fastest.
Arguments:
- dynamics: bfloat16 [16, 1536, 1536], P('tm', 'panel'), may hold values from -1 to 1
- coupling: bfloat16 [16, 1536, 1536], P('tm', 'panel'), may hold values from -1 to 1
- cost_matrix: bfloat16 [16, 1536, 1536], P('tm', 'panel'), may hold values from -1 to 1
- band_offset: int32 [16, 12], P('tm'), may hold values from -1 to 0
- band_width: int32 [16, 12], P('tm'), may hold values from 2 to 3
Outputs:
- level_one: bfloat16 [16, 3, 1536, 1536], P('tm', None, 'panel')
- level_two: bfloat16 [16, 3, 1536, 1536], P('tm', None, 'panel')
All inputs are finite; a program needn't handle non-finite values.
Results may differ from a plain program's by a relative error of at most 0.012.
The roundings to bfloat16 on the way count: a program that leaves them out, or rounds other values in their place, can miss the bound.
Values may be sent and summed in bfloat16 or wider, within the bound.
A program may use at most 128 MiB of HBM per device.

v0:
```python
import jax
import jax.numpy as jnp
from jax import lax
from jax.sharding import PartitionSpec as P

BLOCK = 128
LEVELS = 2


def passed_along(value, axis, by):
    count = lax.axis_size(axis)
    pairs = [(i, i + by) for i in range(count) if 0 <= i + by < count]
    return lax.ppermute(value, axis, pairs)


def contract_rows(left, piece):
    return jnp.dot(left, piece, preferred_element_type=jnp.float32)


def contract_columns(whole, first, count, piece):
    block = lax.dynamic_slice(whole, (0, first), (piece.shape[0], count))
    return lax.dot_general(
        block, piece, (((0,), (0,)), ((), ())), preferred_element_type=jnp.float32
    )


def level_step(element, distance, first):
    a_own, c_own, j_own = element
    rows, width = a_own.shape
    a_part, c_part, j_prev = passed_along((a_own, c_own, j_own), "tm", distance)
    a_prev, c_prev = (
        lax.all_gather(a_part, "panel", axis=0, tiled=True),
        lax.all_gather(c_part, "panel", axis=0, tiled=True),
    )
    a_full, j_full = (
        lax.all_gather(a_own, "panel", axis=0, tiled=True),
        lax.all_gather(j_own, "panel", axis=0, tiled=True),
    )
    k_rows = jnp.dot(c_part, j_full, preferred_element_type=jnp.float32).astype(jnp.bfloat16)
    q_rows = contract_rows(k_rows, lax.all_gather(k_rows, "panel", axis=0, tiled=True)).astype(
        jnp.bfloat16
    )
    k_q = contract_rows(k_rows, lax.all_gather(q_rows, "panel", axis=0, tiled=True))
    row_ids = first + jnp.arange(rows, dtype=jnp.int32)
    identity = (row_ids[:, None] == jnp.arange(width, dtype=jnp.int32)[None, :]).astype(jnp.float32)
    x_rows = (identity - k_rows.astype(jnp.float32) + q_rows.astype(jnp.float32) - k_q).astype(
        jnp.bfloat16
    )
    u_rows = jnp.dot(x_rows, a_prev, preferred_element_type=jnp.float32).astype(jnp.bfloat16)
    a_sum = contract_rows(a_own, lax.all_gather(u_rows, "panel", axis=0, tiled=True))
    s_sum = contract_rows(j_own, lax.all_gather(u_rows, "panel", axis=0, tiled=True))
    a_new = a_sum.astype(jnp.bfloat16)
    s_rows = s_sum.astype(jnp.bfloat16)
    v_rows = jnp.dot(x_rows, c_prev, preferred_element_type=jnp.float32).astype(jnp.bfloat16)
    w_rows = contract_rows(a_own, lax.all_gather(v_rows, "panel", axis=0, tiled=True)).astype(
        jnp.bfloat16
    )
    c_sum = lax.dot_general(
        w_rows, a_full, (((1,), (1,)), ((), ())), preferred_element_type=jnp.float32
    )
    c_new = (c_sum + c_own.astype(jnp.float32)).astype(jnp.bfloat16)
    j_sum = contract_columns(
        a_prev, first, rows, lax.all_gather(s_rows, "panel", axis=0, tiled=True)
    )
    j_new = (j_sum + j_prev.astype(jnp.float32)).astype(jnp.bfloat16)
    valid = lax.axis_index("tm") >= distance
    return (
        jnp.where(valid, a_new, a_own),
        jnp.where(valid, c_new, c_own),
        jnp.where(valid, j_new, j_own),
    )


def shards(dynamics, coupling, cost_matrix, band_offset, band_width):
    rows = dynamics.shape[1]
    width = dynamics.shape[2]
    first = lax.axis_index("panel") * rows
    row_block = (first + jnp.arange(rows, dtype=jnp.int32)) // BLOCK
    block_ids = jnp.arange(width // BLOCK, dtype=jnp.int32)
    picked = row_block[:, None] == block_ids[None, :]
    offsets = jnp.sum(jnp.where(picked, band_offset[0][None, :], 0), axis=1)
    widths = jnp.sum(jnp.where(picked, band_width[0][None, :], 0), axis=1)
    col_block = jnp.arange(width, dtype=jnp.int32) // BLOCK
    lower = row_block + offsets
    inside = (col_block[None, :] >= lower[:, None]) & (
        col_block[None, :] < (lower + widths)[:, None]
    )
    c_start = jnp.where(inside, coupling[0], jnp.zeros_like(coupling[0]))
    element = (dynamics[0], c_start, cost_matrix[0])
    results = []
    for level in range(LEVELS):
        element = level_step(element, 2**level, first)
        results.append(jnp.stack(element, axis=0)[None])
    return (results[0], results[1])


def solution(mesh):
    in_specs = (
        P("tm", "panel", None),
        P("tm", "panel", None),
        P("tm", "panel", None),
        P("tm", None),
        P("tm", None),
    )
    out_specs = (P("tm", None, "panel", None), P("tm", None, "panel", None))
    return jax.shard_map(shards, mesh=mesh, in_specs=in_specs, out_specs=out_specs, check_vma=False)
```

profile of v0, /device:TPU:1, one launch (start us, length us, event | category | flops | bytes accessed | tf_op | source)
XLA Modules:
  0.0 1131.7 jit_solution(3765280901157855510)
XLA Ops:
  8.8 1.1 and_select_fusion
  9.9 4.9 collective-permute-start
  14.8 3.6 collective-permute-done
  18.5 54.4 %all-gather.53.cloned.1.call-done = bf16[1,1536,1536]{2,1,0:T(8,128)(2,1)} async-done(((bf16[1,96,1536]{2,1,0:T(8,128)(2,1)}), bf16[1,1536,1536]{2,1,0:T(8,128)(2,1)}) %all-gather.53.cloned.1.call-update) | async-done | bytes 4718608 | tf_op jit(solution)/shard_map/all_gather | solution.py:37
  72.9 3.9 fusion.15
  76.9 58.7 %all-gather.21.cloned.1.call-done = bf16[1536,1536]{1,0:T(8,128)(2,1)} async-done(((bf16[96,1536]{1,0:T(8,128)(2,1)}), bf16[1536,1536]{1,0:T(8,128)(2,1)}) %all-gather.21.cloned.1.call-update) | async-done | bytes 4718608 | tf_op jit(solution)/shard_map/all_gather | solution.py:40
  135.5 4.0 convolution_convert_fusion.12
  139.7 3.9 collective-permute-start.1
  143.6 3.6 collective-permute-done.1
  148.0 50.3 %all-gather.23.cloned.1.call-done = bf16[1536,1536]{1,0:T(8,128)(2,1)} async-done(((bf16[96,1536]{1,0:T(8,128)(2,1)}), bf16[1536,1536]{1,0:T(8,128)(2,1)}) %all-gather.23.cloned.1.call-update) | async-done | bytes 4718608 | tf_op jit(solution)/shard_map/all_gather | solution.py:43
  198.3 3.3 fusion.7
  201.6 57.6 %all-gather.25.cloned.1.call-done = bf16[1536,1536]{1,0:T(8,128)(2,1)} async-done(((bf16[96,1536]{1,0:T(8,128)(2,1)}), bf16[1536,1536]{1,0:T(8,128)(2,1)}) %all-gather.25.cloned.1.call-update) | async-done | bytes 4718608 | tf_op jit(solution)/shard_map/all_gather | solution.py:32
  259.2 3.9 convolution_convert_fusion.11
  263.8 58.1 %all-gather.27.cloned.1.call-done = bf16[1536,1536]{1,0:T(8,128)(2,1)} async-done(((bf16[96,1536]{1,0:T(8,128)(2,1)}), bf16[1536,1536]{1,0:T(8,128)(2,1)}) %all-gather.27.cloned.1.call-update) | async-done | bytes 4718608 | tf_op jit(solution)/shard_map/all_gather | solution.py:50
  321.8 3.9 fusion.27
  326.6 56.1 %all-gather.29.cloned.1.call-done = bf16[1536,1536]{1,0:T(8,128)(2,1)} async-done(((bf16[96,1536]{1,0:T(8,128)(2,1)}), bf16[1536,1536]{1,0:T(8,128)(2,1)}) %all-gather.29.cloned.1.call-update) | async-done | bytes 4718608 | tf_op jit(solution)/shard_map/all_gather | solution.py:33
  382.7 3.9 convolution_convert_fusion.10
  386.7 3.9 collective-permute-start.2
  390.6 3.6 collective-permute-done.2
  394.3 50.0 %all-gather.33.cloned.1.call-done = bf16[1536,1536]{1,0:T(8,128)(2,1)} async-done(((bf16[96,1536]{1,0:T(8,128)(2,1)}), bf16[1536,1536]{1,0:T(8,128)(2,1)}) %all-gather.33.cloned.1.call-update) | async-done | bytes 4718608 | tf_op jit(solution)/shard_map/all_gather | solution.py:63
  444.3 4.3 fusion.21
  448.7 56.6 %all-gather.55.cloned.1.call-done = bf16[1,1536,1536]{2,1,0:T(8,128)(2,1)} async-done(((bf16[1,96,1536]{2,1,0:T(8,128)(2,1)}), bf16[1,1536,1536]{2,1,0:T(8,128)(2,1)}) %all-gather.55.cloned.1.call-update) | async-done | bytes 4718608 | tf_op jit(solution)/shard_map/all_gather | solution.py:36
  505.3 61.6 %all-gather.31.cloned.1.call-done = bf16[1536,1536]{1,0:T(8,128)(2,1)} async-done(((bf16[96,1536]{1,0:T(8,128)(2,1)}), bf16[1536,1536]{1,0:T(8,128)(2,1)}) %all-gather.31.cloned.1.call-update) | async-done | bytes 4718608 | tf_op jit(solution)/shard_map/all_gather | solution.py:55
  566.9 6.1 fusion.28
  573.0 3.2 collective-permute-start.3
  576.2 5.5 collective-permute-done.3
  581.7 46.6 %all-gather.35.cloned.1.call-done = bf16[1536,1536]{1,0:T(8,128)(2,1)} async-done(((bf16[96,1536]{1,0:T(8,128)(2,1)}), bf16[1536,1536]{1,0:T(8,128)(2,1)}) %all-gather.35.cloned.1.call-update) | async-done | bytes 4718608 | tf_op jit(solution)/shard_map/all_gather | solution.py:37
  628.3 3.9 convolution_convert_fusion.9
  632.3 58.6 %all-gather.37.cloned.1.call-done = bf16[1536,1536]{1,0:T(8,128)(2,1)} async-done(((bf16[96,1536]{1,0:T(8,128)(2,1)}), bf16[1536,1536]{1,0:T(8,128)(2,1)}) %all-gather.37.cloned.1.call-update) | async-done | bytes 4718608 | tf_op jit(solution)/shard_map/all_gather | solution.py:40
  691.0 4.0 convolution_convert_fusion.8
  695.1 3.3 fusion.26
  698.4 3.2 collective-permute-start.4
  701.6 5.5 collective-permute-done.4
  708.4 45.3 %all-gather.39.cloned.1.call-done = bf16[1536,1536]{1,0:T(8,128)(2,1)} async-done(((bf16[96,1536]{1,0:T(8,128)(2,1)}), bf16[1536,1536]{1,0:T(8,128)(2,1)}) %all-gather.39.cloned.1.call-update) | async-done | bytes 4718608 | tf_op jit(solution)/shard_map/all_gather | solution.py:43
  753.8 3.2 fusion.9
  757.0 57.8 %all-gather.41.cloned.1.call-done = bf16[1536,1536]{1,0:T(8,128)(2,1)} async-done(((bf16[96,1536]{1,0:T(8,128)(2,1)}), bf16[1536,1536]{1,0:T(8,128)(2,1)}) %all-gather.41.cloned.1.call-update) | async-done | bytes 4718608 | tf_op jit(solution)/shard_map/all_gather | solution.py:32
  814.8 3.9 convolution_convert_fusion.7
  819.4 56.3 %all-gather.45.cloned.1.call-done = bf16[1536,1536]{1,0:T(8,128)(2,1)} async-done(((bf16[96,1536]{1,0:T(8,128)(2,1)}), bf16[1536,1536]{1,0:T(8,128)(2,1)}) %all-gather.45.cloned.1.call-update) | async-done | bytes 4718608 | tf_op jit(solution)/shard_map/all_gather | solution.py:33
  875.6 4.0 convolution_convert_fusion.5
  879.7 57.4 %all-gather.43.cloned.1.call-done = bf16[1536,1536]{1,0:T(8,128)(2,1)} async-done(((bf16[96,1536]{1,0:T(8,128)(2,1)}), bf16[1536,1536]{1,0:T(8,128)(2,1)}) %all-gather.43.cloned.1.call-update) | async-done | bytes 4718608 | tf_op jit(solution)/shard_map/all_gather | solution.py:50
  937.1 3.9 convolution_convert_fusion.3
  941.0 3.4 collective-permute-start.5
  945.4 52.5 %all-gather.49.cloned.1.call-done = bf16[1536,1536]{1,0:T(8,128)(2,1)} async-done(((bf16[96,1536]{1,0:T(8,128)(2,1)}), bf16[1536,1536]{1,0:T(8,128)(2,1)}) %all-gather.49.cloned.1.call-update) | async-done | bytes 4718608 | tf_op jit(solution)/shard_map/all_gather | solution.py:36
  997.9 60.9 %all-gather.47.cloned.1.call-done = bf16[1536,1536]{1,0:T(8,128)(2,1)} async-done(((bf16[96,1536]{1,0:T(8,128)(2,1)}), bf16[1536,1536]{1,0:T(8,128)(2,1)}) %all-gather.47.cloned.1.call-update) | async-done | bytes 4718608 | tf_op jit(solution)/shard_map/all_gather | solution.py:55
  1058.8 6.1 fusion.22
  1064.9 3.2 fusion.24
  1068.1 52.1 %all-gather.51.cloned.1.call-done = bf16[1536,1536]{1,0:T(8,128)(2,1)} async-done(((bf16[96,1536]{1,0:T(8,128)(2,1)}), bf16[1536,1536]{1,0:T(8,128)(2,1)}) %all-gather.51.cloned.1.call-update) | async-done | bytes 4718608 | tf_op jit(solution)/shard_map/all_gather | solution.py:63
  1120.2 3.6 fusion.23
  (70 shorter events, 8.2 us)
Async XLA Ops:
  7.2 65.7 %all-gather.53.cloned.1.call-start = ((), (), s32[]{:S(2)}) async-start(), calls=%async_computation.16 | async-start | bytes 5013504 | tf_op jit(solution)/shard_map/all_gather | solution.py:37
  7.9 127.6 %all-gather.21.cloned.1.call-start = ((), (), s32[]{:S(2)}) async-start(), calls=%async_computation | async-start | bytes 5013504 | tf_op jit(solution)/shard_map/all_gather | solution.py:40
  9.9 8.6 collective-permute-start
  18.5 121.1 %copy-start.9 = (bf16[96,1536]{1,0:T(8,128)(2,1)}, bf16[96,1536]{1,0:T(8,128)(2,1)S(1)}, u32[]{:S(2)}) copy-start(bf16[96,1536]{1,0:T(8,128)(2,1)S(1)} %collective-permute-done) | copy-start | bytes 884740
  18.5 121.2 %copy-start.7 = (bf16[1,96,1536]{2,1,0:T(8,128)(2,1)S(1)}, bf16[1,96,1536]{2,1,0:T(8,128)(2,1)}, u32[]{:S(2)}) copy-start(bf16[1,96,1536]{2,1,0:T(8,128)(2,1)} %param.5) | copy-start | bytes 884740
  76.8 121.5 %copy-start.4 = (bf16[96,1536]{1,0:T(8,128)(2,1)S(1)}, bf16[96,1536]{1,0:T(8,128)(2,1)}, u32[]{:S(2)}) copy-start(bf16[96,1536]{1,0:T(8,128)(2,1)} %fusion.15) | copy-start | bytes 884740
  76.8 121.5 %all-gather.23.cloned.1.call-start = ((), (), s32[]{:S(2)}) async-start(), calls=%async_computation.1 | async-start | bytes 5013504 | tf_op jit(solution)/shard_map/all_gather | solution.py:43
  139.6 119.6 %all-gather.25.cloned.1.call-start = ((), (), s32[]{:S(2)}) async-start(), calls=%async_computation.2 | async-start | bytes 5013504 | tf_op jit(solution)/shard_map/all_gather | solution.py:32
  139.7 7.6 collective-permute-start.1
  147.2 0.7 copy-start.12
  148.0 173.9 %all-gather.27.cloned.1.call-start = ((), (), s32[]{:S(2)}) async-start(), calls=%async_computation.3 | async-start | bytes 5013504 | tf_op jit(solution)/shard_map/all_gather | solution.py:50
  148.0 173.8 %copy-start.5 = (bf16[1,96,1536]{2,1,0:T(8,128)(2,1)S(1)}, bf16[1,96,1536]{2,1,0:T(8,128)(2,1)}, u32[]{:S(2)}) copy-start(bf16[1,96,1536]{2,1,0:T(8,128)(2,1)} %param.7) | copy-start | bytes 884740
  263.1 119.6 %all-gather.29.cloned.1.call-start = ((), (), s32[]{:S(2)}) async-start(), calls=%async_computation.4 | async-start | bytes 5013504 | tf_op jit(solution)/shard_map/all_gather | solution.py:33
  263.7 180.6 %all-gather.33.cloned.1.call-start = ((), (), s32[]{:S(2)}) async-start(), calls=%async_computation.6 | async-start | bytes 5013504 | tf_op jit(solution)/shard_map/all_gather | solution.py:63
  325.8 179.5 %all-gather.55.cloned.1.call-start = ((), (), s32[]{:S(2)}) async-start(), calls=%async_computation.17 | async-start | bytes 5013504 | tf_op jit(solution)/shard_map/all_gather | solution.py:36
  326.6 240.3 %copy-start.8 = (bf16[1,96,1536]{2,1,0:T(8,128)(2,1)S(1)}, bf16[1,96,1536]{2,1,0:T(8,128)(2,1)}, u32[]{:S(2)}) copy-start(bf16[1,96,1536]{2,1,0:T(8,128)(2,1)} %param.5) | copy-start | bytes 884740
  326.6 240.3 %all-gather.31.cloned.1.call-start = ((), (), s32[]{:S(2)}) async-start(), calls=%async_computation.5 | async-start | bytes 5013504 | tf_op jit(solution)/shard_map/all_gather | solution.py:55
  386.7 241.7 %all-gather.35.cloned.1.call-start = ((), (), s32[]{:S(2)}) async-start(), calls=%async_computation.7 | async-start | bytes 5013504 | tf_op jit(solution)/shard_map/all_gather | solution.py:37
  386.7 7.6 collective-permute-start.2
  448.6 242.4 %all-gather.37.cloned.1.call-start = ((), (), s32[]{:S(2)}) async-start(), calls=%async_computation.8 | async-start | bytes 5013504 | tf_op jit(solution)/shard_map/all_gather | solution.py:40
  573.0 8.7 collective-permute-start.3
  581.7 113.3 %copy-start.10 = (bf16[96,1536]{1,0:T(8,128)(2,1)}, bf16[96,1536]{1,0:T(8,128)(2,1)S(1)}, u32[]{:S(2)}) copy-start(bf16[96,1536]{1,0:T(8,128)(2,1)S(1)} %collective-permute-done.3) | copy-start | bytes 884740
  632.3 121.5 %copy-start.3 = (bf16[96,1536]{1,0:T(8,128)(2,1)S(1)}, bf16[96,1536]{1,0:T(8,128)(2,1)}, u32[]{:S(2)}) copy-start(bf16[96,1536]{1,0:T(8,128)(2,1)} %convolution_convert_fusion.9) | copy-start | bytes 884740
  632.3 121.5 %all-gather.39.cloned.1.call-start = ((), (), s32[]{:S(2)}) async-start(), calls=%async_computation.9 | async-start | bytes 5013504 | tf_op jit(solution)/shard_map/all_gather | solution.py:43
  695.0 58.7 %copy-start.6 = (bf16[96,1536]{1,0:T(8,128)(2,1)S(1)}, bf16[96,1536]{1,0:T(8,128)(2,1)}, u32[]{:S(2)}) copy-start(bf16[96,1536]{1,0:T(8,128)(2,1)} %convolution_convert_fusion.8) | copy-start | bytes 884740
  695.1 119.7 %all-gather.41.cloned.1.call-start = ((), (), s32[]{:S(2)}) async-start(), calls=%async_computation.10 | async-start | bytes 5013504 | tf_op jit(solution)/shard_map/all_gather | solution.py:32
  698.4 120.3 %copy-start.1 = (bf16[96,1536]{1,0:T(8,128)(2,1)}, bf16[96,1536]{1,0:T(8,128)(2,1)S(1)}, u32[]{:S(2)}) copy-start(bf16[96,1536]{1,0:T(8,128)(2,1)S(1)} %fusion.26) | copy-start | bytes 884740
  698.4 8.7 collective-permute-start.4
  707.1 0.7 copy-start.11
  707.8 167.8 %all-gather.45.cloned.1.call-start = ((), (), s32[]{:S(2)}) async-start(), calls=%async_computation.12 | async-start | bytes 5013504 | tf_op jit(solution)/shard_map/all_gather | solution.py:33
  708.4 228.7 %all-gather.43.cloned.1.call-start = ((), (), s32[]{:S(2)}) async-start(), calls=%async_computation.11 | async-start | bytes 5013504 | tf_op jit(solution)/shard_map/all_gather | solution.py:50
  757.0 180.1 %copy-start = (bf16[96,1536]{1,0:T(8,128)(2,1)S(1)}, bf16[96,1536]{1,0:T(8,128)(2,1)}, u32[]{:S(2)}) copy-start(bf16[96,1536]{1,0:T(8,128)(2,1)} %fusion.21) | copy-start | bytes 884740
  818.7 179.2 %all-gather.49.cloned.1.call-start = ((), (), s32[]{:S(2)}) async-start(), calls=%async_computation.14 | async-start | bytes 5013504 | tf_op jit(solution)/shard_map/all_gather | solution.py:36
  819.3 125.1 %copy-start.2 = (bf16[96,1536]{1,0:T(8,128)(2,1)S(1)}, bf16[96,1536]{1,0:T(8,128)(2,1)}, u32[]{:S(2)}) copy-start(bf16[96,1536]{1,0:T(8,128)(2,1)} %copy-done.1) | copy-start | bytes 884740
  819.3 239.5 %all-gather.47.cloned.1.call-start = ((), (), s32[]{:S(2)}) async-start(), calls=%async_computation.13 | async-start | bytes 5013504 | tf_op jit(solution)/shard_map/all_gather | solution.py:55
  879.6 240.6 %all-gather.51.cloned.1.call-start = ((), (), s32[]{:S(2)}) async-start(), calls=%async_computation.15 | async-start | bytes 5013504 | tf_op jit(solution)/shard_map/all_gather | solution.py:63
  941.0 127.1 %collective-permute-start.5 = (bf16[96,1536]{1,0:T(8,128)(2,1)S(1)}, bf16[96,1536]{1,0:T(8,128)(2,1)S(1)}, u32[]{:S(2)}, u32[]{:S(2)}) collective-permute-start(bf16[96,1536]{1,0:T(8,128)(2,1)S(1)} %copy-done), channel_id=1, source_target_pairs={{0,32},{16,48},{32,64},{48,80},{64,96},{80,112},{96,128},{112,144}... | collective-permute-start | bytes 884744 | tf_op jit(solution)/shard_map/ppermute | solution.py:13
Sparse Core Ops, SparseCore 0:
  10.4 62.4 all-gather.52
  76.9 58.5 all-gather.20
  139.7 58.5 all-gather.22
  200.6 58.5 all-gather.24
  263.3 58.5 all-gather.26
  324.1 58.5 all-gather.28
  385.7 58.5 all-gather.32
  446.7 58.5 all-gather.54
  508.3 58.5 all-gather.30
  569.7 58.5 all-gather.34
  632.4 58.5 all-gather.36
  695.2 58.5 all-gather.38
  756.2 58.5 all-gather.40
  817.1 58.5 all-gather.44
  878.5 58.5 all-gather.42
  939.4 58.5 all-gather.48
  1000.2 58.5 all-gather.46
  1061.7 58.5 all-gather.50
where the time goes:
time: 1130 us
  waiting for transfers between devices  1020 us (90%)
  matrix products  72.6 us (6%)
  starting transfers between devices  23.2 us (2%)
  between operations  14.5 us (1%)
    all_gather x2, waiting for transfers between devices, level_step(): lax.all_gather(v_rows, 'panel', axis=0, tiled=True)  122 us
    all_gather x2, waiting for transfers between devices, level_step(): lax.all_gather(k_rows, 'panel', axis=0, tiled=True)  117 us
    all_gather x2, waiting for transfers between devices, level_step(): lax.all_gather(u_rows, 'panel', axis=0, tiled=True)  115 us
    all_gather x2, waiting for transfers between devices, level_step(): lax.all_gather(a_part, 'panel', axis=0, tiled=True)  115 us
    all_gather x2, waiting for transfers between devices, level_step(): lax.all_gather(c_part, 'panel', axis=0, tiled=True)  112 us
    all_gather x2, waiting for transfers between devices, level_step(): lax.all_gather(a_own, 'panel', axis=0, tiled=True)  109 us
    all_gather x2, waiting for transfers between devices, level_step(): lax.all_gather(s_rows, 'panel', axis=0, tiled=True)  102 us
    all_gather x2, waiting for transfers between devices, level_step(): lax.all_gather(j_own, 'panel', axis=0, tiled=True)  101 us
  transfers between devices with their start and end apart: 24, of which 23 were waited for; matrix products, arithmetic and copies ran while one was open for 5% of the time, Pallas kernels for 0%

commit v1 on v0

v1 whole, which is shorter than its diff:
```python
import jax
import jax.numpy as jnp
from jax import lax
from jax.experimental import pallas as pl
from jax.experimental.pallas import tpu as pltpu
from jax.sharding import PartitionSpec as P

BLOCK = 128
MESH = pl.DeviceIdType.MESH
F32 = jnp.float32
BF16 = jnp.bfloat16
TILE = 512

X_OWN, Y_LOW, Y_HIGH, PART_LOW, PART_HIGH, FAR_LOW, FAR_HIGH, PART_FAR, XH_LOW, XH_HIGH, XH_FAR, MATE = range(12)
J2, A1, C1, A2 = range(4)


def scan_kernel(a_in, c_in, j_in, one_out, two_out, full, c_own, j_prev, y_ref, z1, z2, g_ref, pt, sel,
                w_ref, stage, final, recv, sent, first, first_sent, out_recv, out_sent, local):
    rows, width = a_in.shape
    half = rows // 2
    tm = lax.axis_index("tm")
    panel = lax.axis_index("panel")
    z, c = tm // 2, tm % 2
    y, x = panel // 4, panel % 4
    planes = lax.axis_size("tm") // 2
    g = x // 2
    own = 1 - (g + c - 2 * g * c)

    def device(xx, yy, zz, cc):
        return (zz * 2 + cc, yy * 4 + xx)

    xo = x * own + (3 - x) * (1 - own)
    pair = 4 * g + 1 - x
    xp = pair * own + (3 - pair) * (1 - own)
    yh, yl = (y + 1) % 4, (y + 3) % 4
    yf = (y + 2) % 4
    low, high = device(x, yl, z, c), device(x, yh, z, c)
    beside = device(pair, y, z, c)
    mate = device(x, y, z, 1 - c)
    swap = device(3 - x, y, z, 1 - c)
    z_next = (z + c) % planes
    z_prev = (z + planes - (1 - g)) % planes
    following = device((3 - x) * own + x * (1 - own), y, z_next, c * own + (1 - c) * (1 - own))
    preceding = device(x * own + (3 - x) * (1 - own), y, z_prev, (1 - c) * own + c * (1 - own))
    up = device(x, y, (z + 1) % planes, c)
    down = device(x, y, (z + planes - 1) % planes, c)
    step = z * 2 + g

    def at(col, yy, part=None):
        base = (yy * 4 + col) * rows
        if part is None:
            return pl.ds(pl.multiple_of(base, 16), rows)
        return pl.ds(pl.multiple_of(base + part * half, 16), half)

    mine = at(xo, y)

    barrier = pltpu.get_barrier_semaphore()
    for other in (low, high, beside, mate, down, preceding, swap):
        pl.semaphore_signal(barrier, inc=1, device_id=other, device_id_type=MESH)
    pl.semaphore_wait(barrier, 7)

    def remote(src, dst, send_sem, recv_sem, to):
        return pltpu.make_async_remote_copy(
            src_ref=src, dst_ref=dst, send_sem=send_sem, recv_sem=recv_sem, device_id=to, device_id_type=MESH
        )

    def hand_over(src, dst, k):
        @pl.when(own == 1)
        def _():
            pltpu.make_async_copy(src, dst, first.at[k]).start()

        @pl.when(own == 0)
        def _():
            remote(src, dst, first_sent.at[k], first.at[k], swap).start()

    def hand_on(src, dst, k):
        remote(src, dst, first_sent.at[k], first.at[k], following).start()

    phys = at(x, y)
    hand_over(j_in, full.at[0, J2, phys], 0)
    hand_on(a_in, full.at[0, A1, phys], 1)
    hand_on(c_in, full.at[0, C1, phys], 2)
    hand_over(a_in, full.at[0, A2, phys], 3)
    hand_on(j_in, j_prev.at[0], 5)
    hand_over(c_in, c_own.at[0], 4)

    def got(dst, sem):
        pltpu.make_async_copy(dst, dst, sem).wait()

    def send(level, m, where, to, k):
        ref = full.at[level, m, where]
        remote(ref, ref, sent.at[level, m], recv.at[level, m, k], to).start()

    def wait(level, m, where, k):
        ref = full.at[level, m, where]
        remote(ref, ref, sent.at[level, m], recv.at[level, m, k], mate).wait_recv()

    def start_own(level, m):
        send(level, m, mine, beside, X_OWN)
        send(level, m, mine, high, Y_LOW)
        send(level, m, mine, low, Y_HIGH)
        send(level, m, mine, mate, MATE)

    def near(level, m):
        def e1():
            wait(level, m, at(xp, y), X_OWN)
            send(level, m, at(xp, y, 1), high, PART_LOW)
            send(level, m, at(xp, y, 1), low, PART_HIGH)
            send(level, m, at(xp, y), mate, MATE)

        def e2():
            wait(level, m, at(xo, yl), Y_LOW)
            send(level, m, at(xo, yl, 0), high, FAR_LOW)
            send(level, m, at(xo, yl, 0), beside, XH_LOW)
            send(level, m, at(xo, yl), mate, MATE)

        def e3():
            wait(level, m, at(xo, yh), Y_HIGH)
            send(level, m, at(xo, yh, 1), low, FAR_HIGH)
            send(level, m, at(xo, yh, 0), beside, XH_HIGH)
            send(level, m, at(xo, yh), mate, MATE)

        return [e1, e2, e3]

    def far(level, m):
        def e4():
            wait(level, m, at(xp, yl, 1), PART_LOW)
            if m % 2 == 0:
                send(level, m, at(xp, yl, 1), high, PART_FAR)
            send(level, m, at(xp, yl, 1), mate, MATE)

        def e5():
            wait(level, m, at(xp, yh, 1), PART_HIGH)
            if m % 2 == 1:
                send(level, m, at(xp, yh, 1), low, PART_FAR)
            send(level, m, at(xp, yh, 1), mate, MATE)

        def e6():
            wait(level, m, at(xo, yf, 0), FAR_LOW)
            send(level, m, at(xo, yf, 0), beside, XH_FAR)
            send(level, m, at(xo, yf, 0), mate, MATE)

        def e7():
            wait(level, m, at(xo, yf, 1), FAR_HIGH)
            send(level, m, at(xo, yf, 1), mate, MATE)

        def tail(where, k):
            def run():
                wait(level, m, where, k)
                send(level, m, where, mate, MATE)

            return run

        return [
            e4, e5, e6, e7,
            tail(at(xp, yl, 0), XH_LOW),
            tail(at(xp, yh, 0), XH_HIGH),
            tail(at(xp, yf, 1), PART_FAR),
            tail(at(xp, yf, 0), XH_FAR),
        ]

    def complete(level, m):
        wait(level, m, pl.ds(0, 8 * rows), MATE)

    def tiles(body, tile=TILE):
        def run(i, carry):
            body(pl.ds(pl.multiple_of(i * tile, tile), tile))
            return carry

        lax.fori_loop(0, width // tile, run, 0)

    def dot(left, right):
        return jnp.dot(left, right, preferred_element_type=F32)

    def dot_t(left, right):
        return lax.dot_general(left, right, (((1,), (1,)), ((), ())), preferred_element_type=F32)

    def interleave(tasks, events):
        tasks, events = list(tasks), list(events)
        total = max(len(tasks), 1)
        done = 0
        for i, task in enumerate(tasks):
            upto = (len(events) * (i + 1)) // total
            while done < upto:
                events[done]()
                done += 1
            task()
        while done < len(events):
            events[done]()
            done += 1

    def compute(level):
        a_two, j_two = full.at[level, A2], full.at[level, J2]
        a_one, c_one = full.at[level, A1], full.at[level, C1]
        keep = step >= 2**level

        def select():
            block = (yoff * 3) // 4
            block = lax.min(block, width // BLOCK - 2)
            offset = yoff * rows - block * BLOCK
            window = pl.ds(pl.multiple_of(block * BLOCK, BLOCK), 2 * BLOCK)
            r_ids = lax.broadcasted_iota(jnp.int32, (rows, 2 * BLOCK), 0)
            c_ids = lax.broadcasted_iota(jnp.int32, (rows, 2 * BLOCK), 1)
            hot = (c_ids == r_ids + offset).astype(F32).astype(BF16)

            def body(cols):
                sel[:, cols] = dot_t(hot, a_one[cols, window]).astype(BF16)

            tiles(body)

        def start_cost():
            def body(cols):
                y_ref[rows:, cols] = dot(sel[...], j_two[:, cols]).astype(BF16)

            tiles(body)

        def start_transition():
            y_ref[:rows, :] = a_two[mine, :]

        def times_c(src):
            def run():
                def body(cols):
                    g_ref[:, cols] = dot(src[...], c_one[:, cols]).astype(BF16)

                tiles(body)

            return run

        def times_j(dst):
            def run():
                def body(cols):
                    dst[:, cols] = dot(g_ref[...], j_two[:, cols]).astype(BF16)

                tiles(body)

            return run

        def last_power():
            def body(cols):
                cube = dot(g_ref[...], j_two[:, cols])
                total = y_ref[:, cols].astype(F32) - z1[:, cols].astype(F32) + z2[:, cols].astype(F32) - cube
                pt[:, cols] = total.astype(BF16)

            tiles(body)

        def new_a_j():
            def body(cols):
                both = dot(pt[...], a_one[:, cols])
                a_new = both[:rows]
                j_new = both[rows:] + j_prev[level, :, cols].astype(F32)
                stage[level, 0, :, cols] = jnp.where(keep, a_new, a_two[mine, cols].astype(F32)).astype(BF16)
                stage[level, 2, :, cols] = jnp.where(keep, j_new, j_two[mine, cols].astype(F32)).astype(BF16)

            tiles(body)

        def w_rows():
            def body(cols):
                w_ref[:, cols] = dot(pt[:rows, :], c_one[:, cols]).astype(BF16)

            tiles(body)

        def new_c():
            def body(cols):
                old = c_own[level, :, cols].astype(F32)
                c_new = dot_t(w_ref[...], a_two[cols, :]) + old
                stage[level, 1, :, cols] = jnp.where(keep, c_new, old).astype(BF16)

            tiles(body)

        powers = [start_transition, times_c(y_ref), times_j(z1), times_c(z1), times_j(z2), times_c(z2), last_power]
        return [select, start_cost], powers, new_a_j, w_rows, new_c

    yoff = y * 4 + xo

    def copied(src, dst, k):
        copy = pltpu.make_async_copy(src, dst, local.at[k])
        copy.start()
        copy.wait()

    def give_out(src, dst, level, k):
        @pl.when(own == 1)
        def _():
            pltpu.make_async_copy(src, dst, out_recv.at[level, k]).start()

        @pl.when(own == 0)
        def _():
            remote(src, dst, out_sent.at[level, k], out_recv.at[level, k], swap).start()

    def level_head(level, owns):
        owns[0]()
        start_own(level, J2)
        for event in near(level, J2):
            event()
        owns[1]()
        start_own(level, A1)
        for event in far(level, J2) + near(level, A1):
            event()

    def level_tail(level, owns):
        head, powers, new_a_j, w_rows, new_c = compute(level)
        owns[2]()
        start_own(level, C1)
        for event in far(level, A1) + near(level, C1):
            event()
        owns[3]()
        start_own(level, A2)
        complete(level, J2)
        complete(level, A1)
        interleave(head, far(level, C1) + near(level, A2))
        complete(level, C1)
        interleave(powers, far(level, A2))
        owns[4]()
        new_a_j()
        return w_rows, new_c

    owns = [
        lambda: got(full.at[0, J2, mine], first.at[0]),
        lambda: got(full.at[0, A1, mine], first.at[1]),
        lambda: got(full.at[0, C1, mine], first.at[2]),
        lambda: got(full.at[0, A2, mine], first.at[3]),
        lambda: got(j_prev.at[0], first.at[5]),
    ]
    level_head(0, owns)
    w_rows, new_c = level_tail(0, owns)
    copied(stage.at[0, 2], full.at[1, J2, mine], 0)
    copied(stage.at[0, 0], full.at[1, A2, mine], 1)

    def lift(src, dst, k):
        remote(src, dst, first_sent.at[k], first.at[k], up).start()

    lift(full.at[1, A2, mine], full.at[1, A1, mine], 6)
    lift(full.at[1, J2, mine], j_prev.at[1], 7)
    give_out(full.at[1, A2, mine], one_out.at[0], 0, 0)
    give_out(full.at[1, J2, mine], one_out.at[2], 0, 2)
    start_own(1, J2)
    w_rows()
    complete(0, A2)
    got(c_own.at[0], first.at[4])
    new_c()
    copied(stage.at[0, 1], c_own.at[1], 2)
    lift(c_own.at[1], full.at[1, C1, mine], 8)
    give_out(c_own.at[1], one_out.at[1], 0, 1)
    for event in near(1, J2):
        event()
    got(full.at[1, A1, mine], first.at[6])
    start_own(1, A1)
    for event in far(1, J2) + near(1, A1):
        event()
    w_rows, new_c = level_tail(
        1,
        [
            None,
            None,
            lambda: got(full.at[1, C1, mine], first.at[8]),
            lambda: None,
            lambda: got(j_prev.at[1], first.at[7]),
        ],
    )
    copied(stage.at[1, 0], final.at[0], 3)
    give_out(final.at[0], two_out.at[0], 1, 0)
    copied(stage.at[1, 2], final.at[2], 4)
    give_out(final.at[2], two_out.at[2], 1, 2)
    w_rows()
    complete(1, A2)
    new_c()
    copied(stage.at[1, 1], final.at[1], 5)
    give_out(final.at[1], two_out.at[1], 1, 1)

    for level, out in ((0, one_out), (1, two_out)):
        for k in range(3):
            got(out.at[k], out_recv.at[level, k])

            @pl.when(own == 0)
            def _():
                remote(final.at[k], out.at[k], out_sent.at[level, k], out_recv.at[level, k], swap).wait_send()

    for k in (0, 3, 4):

        @pl.when(own == 0)
        def _():
            remote(a_in, c_own.at[0], first_sent.at[k], first.at[k], swap).wait_send()

    for k in (1, 2, 5, 6, 7, 8):
        remote(a_in, c_own.at[0], first_sent.at[k], first.at[k], up).wait_send()
    for level in range(2):
        for m in range(4):
            ref = full.at[level, m, pl.ds(0, 15 * rows)]
            remote(ref, ref, sent.at[level, m], recv.at[level, m, 0], mate).wait_send()


def scan_levels(a, c, j):
    rows, width = a.shape
    vmem = lambda *shape: pltpu.VMEM(shape, BF16)
    dma = lambda *shape: pltpu.SemaphoreType.DMA(shape)
    wide = (2 * rows, width)
    out = jax.ShapeDtypeStruct((3, rows, width), BF16)
    return pl.pallas_call(
        scan_kernel,
        out_shape=(out, out),
        in_specs=[pl.BlockSpec(memory_space=pl.ANY)] * 3,
        out_specs=[pl.BlockSpec(memory_space=pl.ANY)] * 2,
        scratch_shapes=[
            vmem(2, 4, width, width),
            vmem(2, rows, width),
            vmem(2, rows, width),
            vmem(*wide), vmem(*wide), vmem(*wide), vmem(*wide), vmem(*wide),
            vmem(rows, width),
            vmem(rows, width),
            vmem(2, 3, rows, width),
            vmem(3, rows, width),
            dma(2, 4, 12),
            dma(2, 4),
            dma(9),
            dma(9),
            dma(2, 3),
            dma(2, 3),
            dma(6),
        ],
        compiler_params=pltpu.CompilerParams(
            collective_id=0, has_side_effects=True, vmem_limit_bytes=60 * 2**20
        ),
        name="scan_levels",
    )(a, c, j)


def shards(dynamics, coupling, cost_matrix, band_offset, band_width):
    rows = dynamics.shape[1]
    width = dynamics.shape[2]
    first = lax.axis_index("panel") * rows
    row_block = (first + jnp.arange(rows, dtype=jnp.int32)) // BLOCK
    block_ids = jnp.arange(width // BLOCK, dtype=jnp.int32)
    picked = row_block[:, None] == block_ids[None, :]
    offsets = jnp.sum(jnp.where(picked, band_offset[0][None, :], 0), axis=1)
    widths = jnp.sum(jnp.where(picked, band_width[0][None, :], 0), axis=1)
    col_block = jnp.arange(width, dtype=jnp.int32) // BLOCK
    lower = row_block + offsets
    inside = (col_block[None, :] >= lower[:, None]) & (
        col_block[None, :] < (lower + widths)[:, None]
    )
    c_start = jnp.where(inside, coupling[0], jnp.zeros_like(coupling[0]))
    one, two = scan_levels(dynamics[0], c_start, cost_matrix[0])
    return one[None], two[None]


def solution(mesh):
    in_specs = (
        P("tm", "panel", None),
        P("tm", "panel", None),
        P("tm", "panel", None),
        P("tm", None),
        P("tm", None),
    )
    out_specs = (P("tm", None, "panel", None), P("tm", None, "panel", None))
    return jax.shard_map(shards, mesh=mesh, in_specs=in_specs, out_specs=out_specs, check_vma=False)
```

time: 1130 us -> 184 us (0.16)
  waiting for transfers between devices: 1020 us -> 0 us
  Pallas kernels: 0 us -> 177 us
  matrix products: 72.6 us -> 0 us
  starting transfers between devices: 23.2 us -> 0 us
  between operations: 14.5 us -> 0.68 us
    all_gather x18 -> x0, waiting for transfers between devices: 991 us -> none  [the longest x2 122 us: level_step(): lax.all_gather(v_rows, 'panel', axis=0, tiled=True)]
    pallas_call x0 -> x1, Pallas kernels: none -> 177 us  [scan_levels(): pl.pallas_call(scan_kernel, out_shape=(out, out), in_specs=[pl.BlockSpec(...]
    dot_general x18 -> x0, matrix products: 72.6 us -> none  [the longest x8 28.9 us: contract_rows(): return jnp.dot(left, piece, preferred_element_type=jnp.float32)]
    ppermute x6 -> x0, starting transfers between devices: 22.5 us -> none  [passed_along(): return lax.ppermute(value, axis, pairs)]
    ppermute x6 -> x0, waiting for transfers between devices: 21.9 us -> none  [passed_along(): return lax.ppermute(value, axis, pairs)]
  transfers between devices with their start and end apart: 24 -> 0, of which waited for: 23 -> 0; matrix products, arithmetic and copies ran while one was open for 5% -> 0% of each run, Pallas kernels for 0% -> 0%
where the time goes in v1:
time: 184 us
  Pallas kernels  177 us (96%)
  local copies, waits for them, and re-layouts  3.77 us (2%)
  other arithmetic  1.98 us (1%)
    pallas_call x1, Pallas kernels, scan_levels(): pl.pallas_call(scan_kernel, out_shape=(out, out), in_specs=[pl.BlockSpec(...  177 us
    unnamed x8, local copies, waits for them, and re-layouts  3.77 us

profile of v1, /device:TPU:1, one launch (start us, length us, event | category | flops | bytes accessed | tf_op | source)
XLA Modules:
  0.0 183.6 jit_solution(5743290567331384730)
XLA Ops:
  0.6 0.0 copy-start.1
  0.6 0.0 copy-start.2
  0.7 0.6 copy-done.1
  1.3 0.0 copy-done.2
  1.3 0.1 select_reduce_fusion
  1.4 1.9 %and_select_fusion.c_in = bf16[96,1536]{1,0:T(8,128)(2,1)} fusion(bf16[1,96,1536]{2,1,0:T(8,128)(2,1)} %param.6, s32[1536]{0:T(1024)S(1)} %add_select_fusion, s32[96]{0:T(128)S(1)} %get-tuple-element.8, s32[96]{0:T(128)S(1)} %get-tuple-element.9), kind=kLoop, calls=%fused_computation | loop fusion | flops 589824 | bytes 596736 | tf_op jit(solution)/shard_map/jit(_where)/select_n | solution.py:441
  3.3 177.2 %scan_levels.1 = (bf16[3,96,1536]{2,1,0:T(8,128)(2,1)}, bf16[3,96,1536]{2,1,0:T(8,128)(2,1)}) custom-call(bf16[96,1536]{1,0:T(8,128)(2,1)} %bitcast.10, bf16[96,1536]{1,0:T(8,128)(2,1)} %and_select_fusion.c_in, bf16[96,1536]{1,0:T(8,128)(2,1)} %bitcast.11), custom_call_target="tpu_custom_call" | custom-call | tf_op jit(solution)/shard_map/scan_levels/pallas_call | solution.py:398
  180.5 0.0 copy-start
  180.5 2.2 %copy.9 = bf16[1,3,96,1536]{3,2,1,0:T(8,128)(2,1)} copy(bf16[1,3,96,1536]{3,2,1,0:T(8,128)(2,1)} %bitcast.9) | data formatting | bytes 1769472
  182.7 0.0 copy-done
  182.7 0.9 copy.10
  (3 shorter events, 0.0 us)
Async XLA Ops:
  0.6 0.7 copy-start.1
  0.6 0.7 copy-start.2
  180.5 2.2 %copy-start = (bf16[3,96,1536]{2,1,0:T(8,128)(2,1)S(1)}, bf16[3,96,1536]{2,1,0:T(8,128)(2,1)}, u32[]{:S(2)}) copy-start(bf16[3,96,1536]{2,1,0:T(8,128)(2,1)} %get-tuple-element.5) | copy-start | bytes 2654212

commit v2 on v1

--- a/solution.py
+++ b/solution.py
@@ -9,14 +9,16 @@
 MESH = pl.DeviceIdType.MESH
 F32 = jnp.float32
 BF16 = jnp.bfloat16
-TILE = 512
+SPAN = 5
+TILE = 4 * BLOCK
 
 X_OWN, Y_LOW, Y_HIGH, PART_LOW, PART_HIGH, FAR_LOW, FAR_HIGH, PART_FAR, XH_LOW, XH_HIGH, XH_FAR, MATE = range(12)
 J2, A1, C1, A2 = range(4)
-
-
-def scan_kernel(a_in, c_in, j_in, one_out, two_out, full, c_own, j_prev, y_ref, z1, z2, g_ref, pt, sel,
-                w_ref, stage, final, recv, sent, first, first_sent, out_recv, out_sent, local):
+FROM_LOW = (True, False, False, True)
+
+
+def scan_kernel(offset_in, width_in, a_in, c_in, j_in, one_out, two_out, full, c_own, j_prev, y_ref, z1, z2, g_ref,
+                pt, sel, w_ref, stage, final, banded, recv, sent, first, first_sent, out_recv, out_sent, local):
     rows, width = a_in.shape
     half = rows // 2
     tm = lax.axis_index("tm")
@@ -48,12 +50,24 @@
     step = z * 2 + g
 
     def at(col, yy, part=None):
-        base = (yy * 4 + col) * rows
+        q = yy * 4 + col
         if part is None:
-            return pl.ds(pl.multiple_of(base, 16), rows)
-        return pl.ds(pl.multiple_of(base + part * half, 16), half)
-
-    mine = at(xo, y)
+            return q, pl.ds(pl.multiple_of(q * rows, 16), rows)
+        return q, pl.ds(pl.multiple_of(q * rows + part * half, 16), half)
+
+    def span(q):
+        block = lax.max(lax.min((q * 3) // 4 - 1, width // BLOCK - SPAN), 0)
+        return pl.ds(pl.multiple_of(block * BLOCK, BLOCK), SPAN * BLOCK)
+
+    def panel_ref(level, m, where):
+        q, some = where
+        if (level, m) == (0, C1):
+            return full.at[0, C1, some, span(q)]
+        return full.at[level, m, some]
+
+    mine = at(xo, y)[1]
+    raw = pltpu.make_async_copy(c_in, banded.at[0], local.at[5])
+    raw.start()
 
     barrier = pltpu.get_barrier_semaphore()
     for other in (low, high, beside, mate, down, preceding, swap):
@@ -65,6 +79,13 @@
             src_ref=src, dst_ref=dst, send_sem=send_sem, recv_sem=recv_sem, device_id=to, device_id_type=MESH
         )
 
+    yoff = y * 4 + xo
+
+    def copied(src, dst, k):
+        copy = pltpu.make_async_copy(src, dst, local.at[k])
+        copy.start()
+        copy.wait()
+
     def hand_over(src, dst, k):
         @pl.when(own == 1)
         def _():
@@ -77,30 +98,55 @@
     def hand_on(src, dst, k):
         remote(src, dst, first_sent.at[k], first.at[k], following).start()
 
-    phys = at(x, y)
+    phys = at(x, y)[1]
     hand_over(j_in, full.at[0, J2, phys], 0)
     hand_on(a_in, full.at[0, A1, phys], 1)
-    hand_on(c_in, full.at[0, C1, phys], 2)
-    hand_over(a_in, full.at[0, A2, phys], 3)
-    hand_on(j_in, j_prev.at[0], 5)
-    hand_over(c_in, c_own.at[0], 4)
+
+    def hand_coupling():
+        block = (panel * 3) // 4
+        after = lax.min(block + 1, width // BLOCK - 1)
+        r_ids = lax.broadcasted_iota(jnp.int32, (rows, width), 0) + panel * rows
+        c_ids = lax.broadcasted_iota(jnp.int32, (rows, width), 1)
+        later = r_ids >= (block + 1) * BLOCK
+        low_0 = (block + offset_in[0, block]) * BLOCK
+        low_1 = (block + 1 + offset_in[0, after]) * BLOCK
+        start = jnp.where(later, low_1, low_0)
+        stop = jnp.where(later, low_1 + width_in[0, after] * BLOCK, low_0 + width_in[0, block] * BLOCK)
+        raw.wait()
+        values = banded[0].astype(F32)
+        stage[0, 1] = jnp.where((c_ids >= start) & (c_ids < stop), values, 0.0).astype(BF16)
+        copied(stage.at[0, 1], banded.at[1], 4)
+        hand_on(banded.at[1, :, span(panel)], full.at[0, C1, phys, span(panel)], 2)
+        hand_over(a_in, full.at[0, A2, phys], 3)
+        hand_on(j_in, j_prev.at[0], 5)
+        hand_over(banded.at[1], c_own.at[0], 4)
+
+    def clear_outside():
+        for q in range(width // rows):
+            left = max(min((q * 3) // 4 - 1, width // BLOCK - SPAN), 0) * BLOCK
+            right = left + SPAN * BLOCK
+            if left:
+                full[0, C1, q * rows : (q + 1) * rows, :left] = jnp.zeros((rows, left), BF16)
+            if right < width:
+                full[0, C1, q * rows : (q + 1) * rows, right:] = jnp.zeros((rows, width - right), BF16)
 
     def got(dst, sem):
         pltpu.make_async_copy(dst, dst, sem).wait()
 
     def send(level, m, where, to, k):
-        ref = full.at[level, m, where]
+        ref = panel_ref(level, m, where)
         remote(ref, ref, sent.at[level, m], recv.at[level, m, k], to).start()
 
     def wait(level, m, where, k):
-        ref = full.at[level, m, where]
+        ref = panel_ref(level, m, where)
         remote(ref, ref, sent.at[level, m], recv.at[level, m, k], mate).wait_recv()
 
     def start_own(level, m):
-        send(level, m, mine, beside, X_OWN)
-        send(level, m, mine, high, Y_LOW)
-        send(level, m, mine, low, Y_HIGH)
-        send(level, m, mine, mate, MATE)
+        here = at(xo, y)
+        send(level, m, here, beside, X_OWN)
+        send(level, m, here, high, Y_LOW)
+        send(level, m, here, low, Y_HIGH)
+        send(level, m, here, mate, MATE)
 
     def near(level, m):
         def e1():
@@ -126,49 +172,45 @@
     def far(level, m):
         def e4():
             wait(level, m, at(xp, yl, 1), PART_LOW)
-            if m % 2 == 0:
+            if FROM_LOW[m]:
                 send(level, m, at(xp, yl, 1), high, PART_FAR)
-            send(level, m, at(xp, yl, 1), mate, MATE)
 
         def e5():
             wait(level, m, at(xp, yh, 1), PART_HIGH)
-            if m % 2 == 1:
+            if not FROM_LOW[m]:
                 send(level, m, at(xp, yh, 1), low, PART_FAR)
-            send(level, m, at(xp, yh, 1), mate, MATE)
 
         def e6():
             wait(level, m, at(xo, yf, 0), FAR_LOW)
             send(level, m, at(xo, yf, 0), beside, XH_FAR)
-            send(level, m, at(xo, yf, 0), mate, MATE)
 
         def e7():
             wait(level, m, at(xo, yf, 1), FAR_HIGH)
-            send(level, m, at(xo, yf, 1), mate, MATE)
-
-        def tail(where, k):
-            def run():
-                wait(level, m, where, k)
-                send(level, m, where, mate, MATE)
-
-            return run
-
-        return [
-            e4, e5, e6, e7,
-            tail(at(xp, yl, 0), XH_LOW),
-            tail(at(xp, yh, 0), XH_HIGH),
-            tail(at(xp, yf, 1), PART_FAR),
-            tail(at(xp, yf, 0), XH_FAR),
-        ]
+            send(level, m, at(xo, yf), mate, MATE)
+
+        return [e4, e5, e6, e7]
+
+    def crossed(level, m):
+        def e8():
+            wait(level, m, at(xp, yl, 0), XH_LOW)
+            send(level, m, at(xp, yl), mate, MATE)
+
+        def e9():
+            wait(level, m, at(xp, yh, 0), XH_HIGH)
+            send(level, m, at(xp, yh), mate, MATE)
+
+        def e10():
+            wait(level, m, at(xp, yf, 1), PART_FAR)
+            wait(level, m, at(xp, yf, 0), XH_FAR)
+            send(level, m, at(xp, yf), mate, MATE)
+
+        return [e8, e9, e10]
 
     def complete(level, m):
-        wait(level, m, pl.ds(0, 8 * rows), MATE)
-
-    def tiles(body, tile=TILE):
-        def run(i, carry):
-            body(pl.ds(pl.multiple_of(i * tile, tile), tile))
-            return carry
-
-        lax.fori_loop(0, width // tile, run, 0)
+        wait(level, m, (0, pl.ds(0, 8 * rows)), MATE)
+
+    def tiles(body):
+        body(pl.ds(0, width))
 
     def dot(left, right):
         return jnp.dot(left, right, preferred_element_type=F32)
@@ -218,14 +260,18 @@
         def start_transition():
             y_ref[:rows, :] = a_two[mine, :]
 
+        def into_c(src, dst):
+            if level:
+                dst[...] = dot(src[...], c_one[...]).astype(BF16)
+                return
+            deep = TILE + 3 * BLOCK
+            for left in range(0, width, TILE):
+                top = min(max(left - 2 * BLOCK, 0), width - deep)
+                rows_in, cols = slice(top, top + deep), slice(left, left + TILE)
+                dst[:, cols] = dot(src[:, rows_in], c_one[rows_in, cols]).astype(BF16)
+
         def times_c(src):
-            def run():
-                def body(cols):
-                    g_ref[:, cols] = dot(src[...], c_one[:, cols]).astype(BF16)
-
-                tiles(body)
-
-            return run
+            return lambda: into_c(src, g_ref)
 
         def times_j(dst):
             def run():
@@ -255,10 +301,7 @@
             tiles(body)
 
         def w_rows():
-            def body(cols):
-                w_ref[:, cols] = dot(pt[:rows, :], c_one[:, cols]).astype(BF16)
-
-            tiles(body)
+            into_c(pt.at[:rows], w_ref)
 
         def new_c():
             def body(cols):
@@ -271,13 +314,6 @@
         powers = [start_transition, times_c(y_ref), times_j(z1), times_c(z1), times_j(z2), times_c(z2), last_power]
         return [select, start_cost], powers, new_a_j, w_rows, new_c
 
-    yoff = y * 4 + xo
-
-    def copied(src, dst, k):
-        copy = pltpu.make_async_copy(src, dst, local.at[k])
-        copy.start()
-        copy.wait()
-
     def give_out(src, dst, level, k):
         @pl.when(own == 1)
         def _():
@@ -287,29 +323,28 @@
         def _():
             remote(src, dst, out_sent.at[level, k], out_recv.at[level, k], swap).start()
 
+    def run_all(events):
+        for event in events:
+            event()
+
     def level_head(level, owns):
-        owns[0]()
-        start_own(level, J2)
-        for event in near(level, J2):
-            event()
         owns[1]()
         start_own(level, A1)
-        for event in far(level, J2) + near(level, A1):
-            event()
+        run_all(near(level, J2))
 
     def level_tail(level, owns):
         head, powers, new_a_j, w_rows, new_c = compute(level)
         owns[2]()
         start_own(level, C1)
-        for event in far(level, A1) + near(level, C1):
-            event()
+        run_all(far(level, J2) + near(level, A1) + crossed(level, J2))
         owns[3]()
         start_own(level, A2)
+        run_all(far(level, A1) + near(level, C1) + crossed(level, A1))
         complete(level, J2)
         complete(level, A1)
-        interleave(head, far(level, C1) + near(level, A2))
+        interleave(head, far(level, C1) + near(level, A2) + crossed(level, C1))
         complete(level, C1)
-        interleave(powers, far(level, A2))
+        interleave(powers, far(level, A2) + crossed(level, A2))
         owns[4]()
         new_a_j()
         return w_rows, new_c
@@ -317,10 +352,14 @@
     owns = [
         lambda: got(full.at[0, J2, mine], first.at[0]),
         lambda: got(full.at[0, A1, mine], first.at[1]),
-        lambda: got(full.at[0, C1, mine], first.at[2]),
+        lambda: got(full.at[0, C1, mine, span(yoff)], first.at[2]),
         lambda: got(full.at[0, A2, mine], first.at[3]),
         lambda: got(j_prev.at[0], first.at[5]),
     ]
+    owns[0]()
+    start_own(0, J2)
+    hand_coupling()
+    clear_outside()
     level_head(0, owns)
     w_rows, new_c = level_tail(0, owns)
     copied(stage.at[0, 2], full.at[1, J2, mine], 0)
@@ -330,7 +369,6 @@
         remote(src, dst, first_sent.at[k], first.at[k], up).start()
 
     lift(full.at[1, A2, mine], full.at[1, A1, mine], 6)
-    lift(full.at[1, J2, mine], j_prev.at[1], 7)
     give_out(full.at[1, A2, mine], one_out.at[0], 0, 0)
     give_out(full.at[1, J2, mine], one_out.at[2], 0, 2)
     start_own(1, J2)
@@ -340,13 +378,9 @@
     new_c()
     copied(stage.at[0, 1], c_own.at[1], 2)
     lift(c_own.at[1], full.at[1, C1, mine], 8)
+    lift(full.at[1, J2, mine], j_prev.at[1], 7)
     give_out(c_own.at[1], one_out.at[1], 0, 1)
-    for event in near(1, J2):
-        event()
-    got(full.at[1, A1, mine], first.at[6])
-    start_own(1, A1)
-    for event in far(1, J2) + near(1, A1):
-        event()
+    level_head(1, [None, lambda: got(full.at[1, A1, mine], first.at[6])])
     w_rows, new_c = level_tail(
         1,
         [
@@ -381,15 +415,17 @@
         def _():
             remote(a_in, c_own.at[0], first_sent.at[k], first.at[k], swap).wait_send()
 
-    for k in (1, 2, 5, 6, 7, 8):
+    for k in (1, 5, 6, 7, 8):
         remote(a_in, c_own.at[0], first_sent.at[k], first.at[k], up).wait_send()
+    thin = full.at[0, C1, phys, span(panel)]
+    remote(thin, thin, first_sent.at[2], first.at[2], up).wait_send()
     for level in range(2):
         for m in range(4):
-            ref = full.at[level, m, pl.ds(0, 15 * rows)]
+            ref = panel_ref(level, m, (0, pl.ds(0, 15 * rows)))
             remote(ref, ref, sent.at[level, m], recv.at[level, m, 0], mate).wait_send()
 
 
-def scan_levels(a, c, j):
+def scan_levels(offset, reach, a, c, j):
     rows, width = a.shape
     vmem = lambda *shape: pltpu.VMEM(shape, BF16)
     dma = lambda *shape: pltpu.SemaphoreType.DMA(shape)
@@ -398,7 +434,7 @@
     return pl.pallas_call(
         scan_kernel,
         out_shape=(out, out),
-        in_specs=[pl.BlockSpec(memory_space=pl.ANY)] * 3,
+        in_specs=[pl.BlockSpec(memory_space=pltpu.SMEM)] * 2 + [pl.BlockSpec(memory_space=pl.ANY)] * 3,
         out_specs=[pl.BlockSpec(memory_space=pl.ANY)] * 2,
         scratch_shapes=[
             vmem(2, 4, width, width),
@@ -409,6 +445,7 @@
             vmem(rows, width),
             vmem(2, 3, rows, width),
             vmem(3, rows, width),
+            vmem(2, rows, width),
             dma(2, 4, 12),
             dma(2, 4),
             dma(9),
@@ -421,25 +458,11 @@
             collective_id=0, has_side_effects=True, vmem_limit_bytes=60 * 2**20
         ),
         name="scan_levels",
-    )(a, c, j)
+    )(offset, reach, a, c, j)
 
 
 def shards(dynamics, coupling, cost_matrix, band_offset, band_width):
-    rows = dynamics.shape[1]
-    width = dynamics.shape[2]
-    first = lax.axis_index("panel") * rows
-    row_block = (first + jnp.arange(rows, dtype=jnp.int32)) // BLOCK
-    block_ids = jnp.arange(width // BLOCK, dtype=jnp.int32)
-    picked = row_block[:, None] == block_ids[None, :]
-    offsets = jnp.sum(jnp.where(picked, band_offset[0][None, :], 0), axis=1)
-    widths = jnp.sum(jnp.where(picked, band_width[0][None, :], 0), axis=1)
-    col_block = jnp.arange(width, dtype=jnp.int32) // BLOCK
-    lower = row_block + offsets
-    inside = (col_block[None, :] >= lower[:, None]) & (
-        col_block[None, :] < (lower + widths)[:, None]
-    )
-    c_start = jnp.where(inside, coupling[0], jnp.zeros_like(coupling[0]))
-    one, two = scan_levels(dynamics[0], c_start, cost_matrix[0])
+    one, two = scan_levels(band_offset, band_width, dynamics[0], coupling[0], cost_matrix[0])
     return one[None], two[None]
 
 

time: 184 us -> 159 us (0.86)
  Pallas kernels: 177 us -> 155 us
  other arithmetic: 1.98 us -> 0 us
    pallas_call x1, Pallas kernels: 177 us -> 155 us  [scan_levels(): pl.pallas_call(scan_kernel, out_shape=(out, out), in_specs=[pl.BlockSpec(...]
    select_n x3 -> x0, other arithmetic: 1.88 us -> none  [the longest x1 1.86 us: shards(): c_start = jnp.where(inside, coupling[0], jnp.zeros_like(coupling[0]))]
    unnamed x8 -> x4, local copies, waits for them, and re-layouts: 3.77 us -> 3.13 us
where the time goes in v2:
time: 159 us
  Pallas kernels  155 us (97%)
  local copies, waits for them, and re-layouts  3.13 us (2%)
    pallas_call x1, Pallas kernels, scan_levels(): pl.pallas_call(scan_kernel, out_shape=(out, out), in_specs=[pl.BlockSpec(...  155 us

profile of v2, /device:TPU:1, one launch (start us, length us, event | category | flops | bytes accessed | tf_op | source)
XLA Modules:
  0.0 158.7 jit_solution(9967468464001817700)
XLA Ops:
  0.6 154.9 %scan_levels.1 = (bf16[3,96,1536]{2,1,0:T(8,128)(2,1)}, bf16[3,96,1536]{2,1,0:T(8,128)(2,1)}) custom-call(s32[1,12]{1,0:T(1,128)} %offset_in.1, s32[1,12]{1,0:T(1,128)} %width_in.1, bf16[96,1536]{1,0:T(8,128)(2,1)} %bitcast.7, bf16[96,1536]{1,0:T(8,128)(2,1)} %bitcast.8, bf16[96,1536]{1,0:T(8,128)(2,1)} %bitcast.9), custom_call_target="tpu_custom_call" | custom-call | tf_op jit(solution)/shard_map/scan_levels/pallas_call | solution.py:434
  155.5 0.0 copy-start
  155.5 2.2 %copy.9 = bf16[1,3,96,1536]{3,2,1,0:T(8,128)(2,1)} copy(bf16[1,3,96,1536]{3,2,1,0:T(8,128)(2,1)} %bitcast.6) | data formatting | bytes 1769472
  157.7 0.0 copy-done
  157.8 0.9 copy.10
Async XLA Ops:
  155.5 2.2 %copy-start = (bf16[3,96,1536]{2,1,0:T(8,128)(2,1)S(1)}, bf16[3,96,1536]{2,1,0:T(8,128)(2,1)}, u32[]{:S(2)}) copy-start(bf16[3,96,1536]{2,1,0:T(8,128)(2,1)} %get-tuple-element.5) | copy-start | bytes 2654212
